TPU v7x, 512 devices: a whole 4x8x8 slice. The times are simulated.
512 devices in a mesh: row: 32 (over z, y_hi), col: 16 (over y_lo, x, core).
Axes of the slice: x: 4, y: 8 (y_hi: 4, y_lo: 2; y = y_hi * 2 + y_lo), z: 8, core: 2. Of those that a mesh axis runs over, the one named last changes fastest.
Arguments:
- inverse_block: bfloat16 [20480, 20480], P('row', 'col')
- factor_cols: bfloat16 [3, 20480, 512], P(None, 'col', 'row'), may hold values from -6 to 6
- occupancy: int32 [3, 160], replicated, may hold values 0 or 1
- row_block: int32 [3, 160], replicated, may hold values from 0 to 159, each once within a row
- coupling: bfloat16 [2, 512, 512], replicated, may hold values from -0.25 to 0.25
- diag_inverse: float32 [3, 512, 512], P(None, None, 'col'), may hold values from -6 to 6
Outputs:
- columns: float32 [3, 20480, 512], P(None, ('row', 'col'))
- diagonals: float32 [3, 512, 512], P(None, None, 'col')
Inputs may be any that keep to these rules, and one draw needn't show every extreme that they name: `row_block`: each row names every one of the 160 row blocks exactly once.
All inputs are finite; a program needn't handle non-finite values.
Results may differ from a plain program's by a relative error of at most 0.0003.
Values may be sent and summed in bfloat16 or wider, within the bound.
A program may use at most 64 MiB of HBM per device.

v0:
```python
import jax
import jax.numpy as jnp
from jax import lax
from jax.sharding import PartitionSpec as P

highest = lax.Precision.HIGHEST


def routed(gathered, occupancy, row_block, nblocks):
    count = gathered.shape[0]
    width_part = gathered.shape[1] // (nblocks * 128)
    blocks = gathered.reshape(count, nblocks, 128, width_part)
    levels = lax.broadcasted_iota(jnp.int32, (count, nblocks, nblocks), 1)
    picks = ((row_block[:, None, :] == levels) & (occupancy[:, None, :] > 0)).astype(jnp.bfloat16)
    placed = jnp.einsum("kqb,kbtx->kxqt", picks, blocks, preferred_element_type=jnp.float32)
    return placed.astype(jnp.bfloat16).reshape(count, width_part, nblocks * 128)


def split_rows(placed, column, row_parts, col_parts, tile):
    count, width_part, total = placed.shape
    span = total // col_parts
    column_part = lax.dynamic_slice_in_dim(placed, column * span, span, 2)
    grid = placed.reshape(count, width_part, row_parts, col_parts, tile)
    mine = lax.dynamic_index_in_dim(grid, column, 3, keepdims=False)
    return (column_part, jnp.transpose(mine, (0, 2, 1, 3)))


def make_term(inverse_block, column_full):
    return lax.dot_general(
        inverse_block, column_full, (((1,), (2,)), ((), ())), preferred_element_type=jnp.float32
    )


def local_step(summed, own_rows, previous, link, diag_part, column, row_first, rows_total):
    if link is None:
        coupled = jnp.zeros_like(summed)
    else:
        coupled = jnp.dot(previous, link.astype(jnp.float32), precision=highest)
    current = -(summed + coupled)
    own = own_rows.astype(jnp.float32)
    inner = jnp.dot(own, current, precision=highest) - jnp.dot(coupled.T, own.T, precision=highest)
    width = summed.shape[1]
    diag_cols = diag_part.shape[1]
    embedded = lax.dynamic_update_slice(
        jnp.zeros((width, width), jnp.float32), diag_part, (0, column * diag_cols)
    )
    return (current, row_first * embedded - inner / rows_total)


def chain_diag(total, chain_prev, link):
    if link is None:
        return total
    link_wide = link.astype(jnp.float32)
    return total + jnp.dot(
        link_wide.T, jnp.dot(chain_prev, link_wide, precision=highest), precision=highest
    )


def per_device(inverse_block, factor_cols, occupancy, row_block, coupling, diag_inverse):
    column = lax.axis_index("col")
    row_first = (lax.axis_index("row") == 0).astype(jnp.float32)
    row_parts = lax.axis_size("row")
    col_parts = lax.axis_size("col")
    local_rows = inverse_block.shape[0]
    rows_total = local_rows * row_parts
    supers, span, width_part = factor_cols.shape
    width = width_part * row_parts
    tile = local_rows // col_parts
    nblocks = occupancy.shape[1]
    diag_cols = diag_inverse.shape[2]
    flat = factor_cols.reshape(supers, span * width_part)
    column_list = []
    partial_list = []
    previous = None
    for position in range(supers):
        gathered = lax.all_gather(flat[position : position + 1], "col", axis=1, tiled=True)
        placed = routed(
            gathered,
            occupancy[position : position + 1],
            row_block[position : position + 1],
            nblocks,
        )
        column_part, outgoing = split_rows(placed, column, row_parts, col_parts, tile)
        column_full = lax.all_gather(column_part, "row", axis=1, tiled=True)
        arrived = lax.all_to_all(outgoing, "row", split_axis=1, concat_axis=1, tiled=True)
        summed = lax.psum_scatter(
            make_term(inverse_block, column_full), "col", scatter_dimension=0, tiled=True
        )
        link = None if position == 0 else coupling[position - 1]
        current, partial_value = local_step(
            summed[:, 0, :],
            arrived.reshape(width, tile),
            previous,
            link,
            diag_inverse[position],
            column,
            row_first,
            rows_total,
        )
        column_list.append(current)
        partial_list.append(partial_value)
        previous = current
    diag_list = []
    totals = lax.psum(jnp.stack(partial_list), ("row", "col"))
    chain_prev = None
    for position in range(supers):
        link = None if position == 0 else coupling[position - 1]
        diag_now = chain_diag(totals[position], chain_prev, link)
        diag_list.append(lax.dynamic_slice_in_dim(diag_now, column * diag_cols, diag_cols, 1))
        chain_prev = diag_now
    diagonals = jnp.stack(diag_list)
    return (jnp.stack(column_list), diagonals)


def solution(mesh):
    in_specs = (P("row", "col"), P(None, "col", "row"), P(), P(), P(), P(None, None, "col"))
    out_specs = (P(None, ("row", "col"), None), P(None, None, "col"))
    return jax.shard_map(
        per_device, mesh=mesh, in_specs=in_specs, out_specs=out_specs, check_vma=False
    )
```

profile of v0, /device:TPU:17, one launch (start us, length us, event | category | flops | bytes accessed | tf_op | source)
XLA Modules:
  0.0 766.2 jit_solution(6525715898854247528)
XLA Ops:
  7.2 0.9 fusion.67
  8.6 24.0 %all_gather.20 = bf16[1,327680]{1,0:T(2,128)(2,1)S(1)} all-gather(bf16[1,20480]{1,0:T(2,128)(2,1)S(1)} %slice.69), channel_id=1, replica_groups=mesh['row'=32,'col'=16] {'col'}, dimensions={1}, use_global_device_ids=true | all-gather | bytes 696320 | tf_op jit(solution)/shard_map/all_gather | solution.py:76
  32.6 14.5 %reduce.3 = bf16[327680]{0:T(1024)(128)(2,1)} reduce(bf16[1,327680]{1,0:T(2,128)(2,1)S(1)} %all_gather.20, bf16[]{:T(256)} %constant.52), dimensions={0}, to_apply=%all_gather.20.reduce_sub_computation | reduce | bytes 1310722 | tf_op jit(solution)/shard_map/all_gather | solution.py:76
  47.1 6.4 reshape.188
  53.6 4.0 copy.64
  58.2 0.6 constant_dynamic-slice_fusion.6
  59.4 22.1 %all_gather.22 = bf16[1,327680]{1,0:T(2,128)(2,1)} all-gather(bf16[1,20480]{1,0:T(2,128)(2,1)S(1)} %slice.74), channel_id=1, replica_groups=mesh['row'=32,'col'=16] {'col'}, dimensions={1}, use_global_device_ids=true | all-gather | bytes 696320 | tf_op jit(solution)/shard_map/all_gather | solution.py:76
  81.5 14.6 %reduce.5 = bf16[327680]{0:T(1024)(128)(2,1)S(1)} reduce(bf16[1,327680]{1,0:T(2,128)(2,1)} %all_gather.22, bf16[]{:T(256)} %constant.52), dimensions={0}, to_apply=%all_gather.22.reduce_sub_computation | reduce | bytes 1310722 | tf_op jit(solution)/shard_map/all_gather | solution.py:76
  96.2 4.9 reshape.191
  101.1 4.9 copy.67
  106.0 1.4 fusion.15
  107.4 1.1 reshape.192
  108.5 1.4 constant_dynamic-slice_fusion.5
  110.4 29.4 %all_gather.18 = bf16[1,327680]{1,0:T(2,128)(2,1)} all-gather(bf16[1,20480]{1,0:T(2,128)(2,1)S(1)} %slice.65), channel_id=1, replica_groups=mesh['row'=32,'col'=16] {'col'}, dimensions={1}, use_global_device_ids=true | all-gather | bytes 696320 | tf_op jit(solution)/shard_map/all_gather | solution.py:76
  139.9 15.5 %reduce.1 = bf16[327680]{0:T(1024)(128)(2,1)} reduce(bf16[1,327680]{1,0:T(2,128)(2,1)} %all_gather.18, bf16[]{:T(256)} %constant.52), dimensions={0}, to_apply=%all_gather.18.reduce_sub_computation | reduce | bytes 1310722 | tf_op jit(solution)/shard_map/all_gather | solution.py:76
  155.3 6.5 reshape.185
  161.9 4.9 copy.61
  166.8 2.3 fusion.13
  169.0 2.2 reshape.186
  171.2 1.4 constant_dynamic-slice_fusion.7
  172.7 3.6 convolution_bitcast_fusion.1
  176.3 3.8 copy.65
  180.2 42.0 %all-gather.8.cloned.1.call-done = bf16[1,512,1280]{2,1,0:T(8,128)(2,1)} async-done(((bf16[1,16,1280]{2,1,0:T(8,128)(2,1)}), bf16[1,512,1280]{2,1,0:T(8,128)(2,1)}) %all-gather.8.cloned.1.call-update) | async-done | bytes 1310736 | tf_op jit(solution)/shard_map/all_gather | solution.py:84
  222.1 3.6 convolution_bitcast_fusion
  225.7 3.8 copy.68
  229.5 76.1 %all-gather.4.cloned.1.call-done = bf16[1,512,1280]{2,1,0:T(8,128)(2,1)} async-done(((bf16[1,16,1280]{2,1,0:T(8,128)(2,1)}), bf16[1,512,1280]{2,1,0:T(8,128)(2,1)}) %all-gather.4.cloned.1.call-update) | async-done | bytes 1310736 | tf_op jit(solution)/shard_map/all_gather | solution.py:84
  305.6 3.6 convolution_bitcast_fusion.2
  309.2 3.9 copy.62
  313.2 4.1 reshape_reshape.10
  317.3 4.1 reshape_reshape.11
  321.4 2.3 constant_dynamic-slice_fusion.2
  323.8 0.8 reshape.211
  324.7 6.9 all-to-all-start.1
  331.6 4.1 reshape_reshape.9
  335.8 0.8 reshape.209
  336.7 4.3 all-to-all-done.1
  340.9 7.4 all-to-all-start.2
  348.3 1.5 constant_dynamic-slice_fusion.4
  350.0 0.8 reshape.213
  350.8 6.8 all-to-all-done.2
  357.7 5.5 all-to-all-start
  363.6 1.3 dynamic-slice.1
  365.7 2.3 dynamic_update_slice.10
  368.1 2.3 dynamic_update_slice.11
  370.5 1.1 copy-done.9
  371.7 2.3 dynamic_update_slice.9
  375.5 78.5 %all-reduce.9.cloned.1.call-done = (f32[640,1,512]{2,1,0:T(1,128)}, f32[640,1,512]{2,1,0:T(1,128)}, f32[640,1,512]{2,1,0:T(1,128)}) async-done(((f32[640,1,512]{2,1,0:T(1,128)}, f32[640,1,512]{2,1,0:T(1,128)}, f32[640,1,512]{2,1,0:T(1,128)}), (f32[640,1,512]{2,1,0:T(1,128)}, f32[640,1,512]{2,1,0:T(1,128)}, f32[640,1,512]{2,1,0:T(1,128)})) %all-reduce.9.cloned.1.call-update) | async-done | bytes 3932176
  454.0 1.0 dynamic-slice_negate_fusion
  455.0 0.9 constant_dynamic-slice_fusion.9
  457.2 0.9 constant_dynamic-slice_fusion.8
  458.1 0.7 fusion.5
  459.4 0.6 copy-done.10
  460.0 0.7 fusion.8
  461.3 0.7 fusion.2
  461.9 2.0 pad_maximum_fusion
  464.0 1.0 fusion.89
  465.0 0.7 pad_maximum_fusion.1
  465.7 284.7 %all-reduce.7.cloned.1.call-done = f32[3,512,512]{2,1,0:T(8,128)} async-done(((f32[3,512,512]{2,1,0:T(8,128)}), f32[3,512,512]{2,1,0:T(8,128)}) %all-reduce.7.cloned.1.call-update) | async-done | bytes 3145744 | tf_op jit(solution)/shard_map/psum | solution.py:104
  750.4 2.2 fusion.16
  752.6 2.3 fusion.9
  754.9 1.0 fusion.19
  756.1 1.1 convolution_bitcast_fusion.3
  757.1 0.7 copy-done.4
  758.6 0.7 pad_maximum_fusion.2
  (74 shorter events, 8.4 us)
Async XLA Ops:
  7.2 165.6 %copy-start = (bf16[640,1280]{1,0:T(8,128)(2,1)S(1)}, bf16[640,1280]{1,0:T(8,128)(2,1)}, u32[]{:S(2)}) copy-start(bf16[640,1280]{1,0:T(8,128)(2,1)} %param.6) | copy-start | bytes 4915204
  7.2 165.5 %all-gather.6.cloned.1.call-start = ((), (), s32[]{:S(2)}) async-start(), calls=%async_computation.4 | async-start | bytes 1351680 | tf_op jit(solution)/shard_map/all_gather | solution.py:84
  53.5 4.0 copy-start.12
  53.5 4.0 copy-start.13
  58.9 163.2 %all-gather.8.cloned.1.call-start = ((), (), s32[]{:S(2)}) async-start(), calls=%async_computation.5 | async-start | bytes 1351680 | tf_op jit(solution)/shard_map/all_gather | solution.py:84
  109.9 195.7 %all-gather.4.cloned.1.call-start = ((), (), s32[]{:S(2)}) async-start(), calls=%async_computation.3 | async-start | bytes 1351680 | tf_op jit(solution)/shard_map/all_gather | solution.py:84
  172.6 281.4 %all-reduce.9.cloned.1.call-start = ((), (), s32[]{:S(2)}) async-start(), calls=%async_computation.7 | async-start | bytes 7864320
  321.4 10.1 %copy-start.3 = (bf16[1,16,160,128]{3,2,1,0:T(8,128)(2,1)S(1)}, bf16[1,16,160,128]{3,2,1,0:T(8,128)(2,1)}, u32[]{:S(2)}) copy-start(bf16[1,16,160,128]{3,2,1,0:T(8,128)(2,1)} %fusion.13) | copy-start | bytes 1966084
  324.7 16.3 %all-to-all-start.1 = ((bf16[32,2,320]{2,1,0:T(2,128)(2,1)}), bf16[32,2,320]{2,1,0:T(2,128)(2,1)S(1)}, u32[]{:S(2)}, u32[]{:S(2)}) async-start(bf16[32,2,320]{2,1,0:T(2,128)(2,1)} %reshape.211), calls=%async_computation.1 | async-start | bytes 98304 | tf_op jit(solution)/shard_map/all_to_all | solution.py:85
  335.7 27.5 %copy-start.11 = (f32[3,512,32]{1,2,0:T(8,128)S(1)}, f32[3,512,32]{1,2,0:T(8,128)}, u32[]{:S(2)}) copy-start(f32[3,512,32]{1,2,0:T(8,128)} %param.11) | copy-start | bytes 589828
  340.9 16.7 %all-to-all-start.2 = ((bf16[32,2,320]{2,1,0:T(2,128)(2,1)}), bf16[32,2,320]{2,1,0:T(2,128)(2,1)S(1)}, u32[]{:S(2)}, u32[]{:S(2)}) async-start(bf16[32,2,320]{2,1,0:T(2,128)(2,1)} %reshape.209), calls=%async_computation.2 | async-start | bytes 98304 | tf_op jit(solution)/shard_map/all_to_all | solution.py:85
  357.7 16.6 %all-to-all-start = ((bf16[32,2,320]{2,1,0:T(2,128)(2,1)}), bf16[32,2,320]{2,1,0:T(2,128)(2,1)S(1)}, u32[]{:S(2)}, u32[]{:S(2)}) async-start(bf16[32,2,320]{2,1,0:T(2,128)(2,1)} %reshape.213), calls=%async_computation | async-start | bytes 98304 | tf_op jit(solution)/shard_map/all_to_all | solution.py:85
  363.1 387.2 %all-reduce.7.cloned.1.call-start = ((), (), s32[]{:S(2)}) async-start(), calls=%async_computation.6 | async-start | bytes 6291456 | tf_op jit(solution)/shard_map/psum | solution.py:104
  368.0 3.5 copy-start.7
  370.5 1.1 copy-start.9
  371.6 84.2 %copy-start.2 = (bf16[2,512,512]{2,1,0:T(8,128)(2,1)S(1)}, bf16[2,512,512]{2,1,0:T(8,128)(2,1)}, u32[]{:S(2)}) copy-start(bf16[2,512,512]{2,1,0:T(8,128)(2,1)} %param.10) | copy-start | bytes 3145732
  374.0 1.0 copy-start.5
  456.2 1.8 copy-start.8
  458.8 1.2 copy-start.10
  460.0 1.2 copy-start.6
  755.9 1.9 copy-start.4
  758.0 1.4 copy-start.1
Sparse Core Ops, SparseCore 0:
  59.0 80.0 all-gather.5
  142.2 79.8 all-gather.7
  225.9 79.7 all-gather.3
  313.3 140.6 all-reduce.8
  464.1 286.2 all-reduce.6
where the time goes:
time: 774 us; the launch traced here: 766 us
  waiting for transfers between devices  492 us (64%)
  local copies, waits for them, and re-layouts  86.9 us (11%)
  blocking collectives  75.5 us (10%)
  other arithmetic  50.2 us (6%)
  matrix products  25.9 us (3%)
  starting transfers between devices  19.9 us (3%)
  between operations  15.2 us (2%)
    psum x1, waiting for transfers between devices, per_device(): totals = lax.psum(jnp.stack(partial_list), ('row', 'col'))  285 us
    all_gather x3, waiting for transfers between devices, per_device(): column_full = lax.all_gather(column_part, 'row', axis=1, tiled=True)  118 us
    unnamed x6, waiting for transfers between devices  78.6 us
    all_gather x3, blocking collectives, per_device(): lax.all_gather(flat[position:position + 1], 'col', axis=1, tiled=True)  75.5 us
    all_gather x3, other arithmetic, per_device(): lax.all_gather(flat[position:position + 1], 'col', axis=1, tiled=True)  44.6 us
    another operation x9, local copies, waits for them, and re-layouts  32 us
    all_to_all x3, starting transfers between devices, per_device(): lax.all_to_all(outgoing, 'row', split_axis=1, concat_axis=1, tiled=True)  19.7 us
  transfers between devices with their start and end apart: 8, of which 6 were waited for; matrix products, arithmetic and copies ran while one was open for 14% of the time, Pallas kernels for 0%

commit v1 on v0

--- a/solution.py
+++ b/solution.py
@@ -82,7 +82,12 @@
         )
         column_part, outgoing = split_rows(placed, column, row_parts, col_parts, tile)
         column_full = lax.all_gather(column_part, "row", axis=1, tiled=True)
-        arrived = lax.all_to_all(outgoing, "row", split_axis=1, concat_axis=1, tiled=True)
+        arrived = jnp.concatenate(
+            lax.all_to_all(
+                jnp.stack(jnp.split(outgoing, lax.axis_size("row"), axis=1)), "row", 0, 0
+            ),
+            axis=1,
+        )
         summed = lax.psum_scatter(
             make_term(inverse_block, column_full), "col", scatter_dimension=0, tiled=True
         )

time: 774 us -> 777 us (level)
  starting transfers between devices: 19.9 us -> 27.7 us
    unnamed x6, waiting for transfers between devices: 78.6 us -> 105 us
    all_gather x3, waiting for transfers between devices: 118 us -> 96.2 us  [per_device(): column_full = lax.all_gather(column_part, 'row', axis=1, tiled=True)]
    another operation x9 -> x13, local copies, waits for them, and re-layouts: 32 us -> 30.7 us
  transfers between devices with their start and end apart: 8 -> 8, of which waited for: 6 -> 5; matrix products, arithmetic and copies ran while one was open for 14% -> 13% of each run, Pallas kernels for 0% -> 0%
where the time goes in v1:
time: 777 us; the launch traced here: 770 us
  waiting for transfers between devices  495 us (64%)
  local copies, waits for them, and re-layouts  86.8 us (11%)
  blocking collectives  72.7 us (9%)
  other arithmetic  48 us (6%)
  starting transfers between devices  27.7 us (4%)
  matrix products  23.9 us (3%)
  between operations  15.5 us (2%)
    psum x1, waiting for transfers between devices, per_device(): totals = lax.psum(jnp.stack(partial_list), ('row', 'col'))  286 us
    unnamed x6, waiting for transfers between devices  105 us
    all_gather x3, waiting for transfers between devices, per_device(): column_full = lax.all_gather(column_part, 'row', axis=1, tiled=True)  96.2 us
    all_gather x3, blocking collectives, per_device(): lax.all_gather(flat[position:position + 1], 'col', axis=1, tiled=True)  72.7 us
    all_gather x3, other arithmetic, per_device(): lax.all_gather(flat[position:position + 1], 'col', axis=1, tiled=True)  43.7 us
    another operation x9, local copies, waits for them, and re-layouts  30.6 us
    all_to_all x3, starting transfers between devices, per_device(): lax.all_to_all(jnp.stack(jnp.split(outgoing, lax.axis_size('row'), axis=1...  27.1 us
  transfers between devices with their start and end apart: 8, of which 5 were waited for; matrix products, arithmetic and copies ran while one was open for 13% of the time, Pallas kernels for 0%

profile of v1, /device:TPU:17, one launch (start us, length us, event | category | flops | bytes accessed | tf_op | source)
XLA Modules:
  0.0 769.8 jit_solution(13061373277158321488)
XLA Ops:
  7.2 0.9 fusion.73
  8.6 24.0 %all_gather.18 = bf16[1,327680]{1,0:T(2,128)(2,1)S(1)} all-gather(bf16[1,20480]{1,0:T(2,128)(2,1)S(1)} %slice.65), channel_id=1, replica_groups=mesh['row'=32,'col'=16] {'col'}, dimensions={1}, use_global_device_ids=true | all-gather | bytes 696320 | tf_op jit(solution)/shard_map/all_gather | solution.py:76
  32.6 14.5 %reduce.1 = bf16[327680]{0:T(1024)(128)(2,1)} reduce(bf16[1,327680]{1,0:T(2,128)(2,1)S(1)} %all_gather.18, bf16[]{:T(256)} %constant.52), dimensions={0}, to_apply=%all_gather.18.reduce_sub_computation | reduce | bytes 1310722 | tf_op jit(solution)/shard_map/all_gather | solution.py:76
  47.1 6.5 reshape.176
  53.5 4.0 copy.2005
  59.4 21.9 %all_gather.20 = bf16[1,327680]{1,0:T(2,128)(2,1)} all-gather(bf16[1,20480]{1,0:T(2,128)(2,1)S(1)} %slice.69), channel_id=1, replica_groups=mesh['row'=32,'col'=16] {'col'}, dimensions={1}, use_global_device_ids=true | all-gather | bytes 696320 | tf_op jit(solution)/shard_map/all_gather | solution.py:76
  81.3 14.6 %reduce.3 = bf16[327680]{0:T(1024)(128)(2,1)S(1)} reduce(bf16[1,327680]{1,0:T(2,128)(2,1)} %all_gather.20, bf16[]{:T(256)} %constant.52), dimensions={0}, to_apply=%all_gather.20.reduce_sub_computation | reduce | bytes 1310722 | tf_op jit(solution)/shard_map/all_gather | solution.py:76
  95.9 5.0 reshape.179
  101.0 4.9 copy.2010
  105.8 1.4 fusion.14
  107.3 1.1 reshape.180
  108.4 1.4 constant_dynamic-slice_fusion.6
  109.8 4.1 reshape_reshape.20
  114.4 26.8 %all_gather.22 = bf16[1,327680]{1,0:T(2,128)(2,1)} all-gather(bf16[1,20480]{1,0:T(2,128)(2,1)S(1)} %slice.74), channel_id=1, replica_groups=mesh['row'=32,'col'=16] {'col'}, dimensions={1}, use_global_device_ids=true | all-gather | bytes 696320 | tf_op jit(solution)/shard_map/all_gather | solution.py:76
  141.1 14.6 %reduce.5 = bf16[327680]{0:T(1024)(128)(2,1)S(1)} reduce(bf16[1,327680]{1,0:T(2,128)(2,1)} %all_gather.22, bf16[]{:T(256)} %constant.52), dimensions={0}, to_apply=%all_gather.22.reduce_sub_computation | reduce | bytes 1310722 | tf_op jit(solution)/shard_map/all_gather | solution.py:76
  155.8 5.0 reshape.182
  160.8 4.9 copy.2017
  165.7 1.4 fusion.15
  167.1 4.1 reshape_reshape.22
  171.2 2.1 constant_dynamic-slice_fusion.2
  173.9 0.8 reshape.197
  174.8 14.7 %all-to-all-start.2 = ((bf16[32,2,320]{2,1,0:T(2,128)(2,1)}), bf16[32,2,320]{2,1,0:T(2,128)(2,1)S(1)}, u32[]{:S(2)}, u32[]{:S(2)}) async-start(bf16[32,2,320]{2,1,0:T(2,128)(2,1)} %reshape.197), calls=%async_computation.2 | async-start | bytes 98304 | tf_op jit(solution)/shard_map/all_to_all | solution.py:86
  189.5 1.1 reshape.183
  190.7 1.4 constant_dynamic-slice_fusion.5
  192.6 4.1 reshape_reshape.18
  196.7 1.5 constant_dynamic-slice_fusion.4
  199.1 2.5 convolution_bitcast_fusion.2
  201.6 2.2 copy.2006
  203.8 17.9 %all-gather.6.cloned.1.call-done = bf16[1,512,1280]{2,1,0:T(8,128)(2,1)} async-done(((bf16[1,16,1280]{2,1,0:T(8,128)(2,1)}), bf16[1,512,1280]{2,1,0:T(8,128)(2,1)}) %all-gather.6.cloned.1.call-update) | async-done | bytes 1310736 | tf_op jit(solution)/shard_map/all_gather | solution.py:84
  221.7 2.5 convolution_bitcast_fusion.1
  224.2 2.1 copy.2011
  226.3 78.3 %all-gather.8.cloned.1.call-done = bf16[1,512,1280]{2,1,0:T(8,128)(2,1)} async-done(((bf16[1,16,1280]{2,1,0:T(8,128)(2,1)}), bf16[1,512,1280]{2,1,0:T(8,128)(2,1)}) %all-gather.8.cloned.1.call-update) | async-done | bytes 1310736 | tf_op jit(solution)/shard_map/all_gather | solution.py:84
  304.6 2.5 convolution_bitcast_fusion
  307.2 2.2 copy.2018
  309.6 0.8 reshape.199
  310.4 6.9 all-to-all-start.1
  317.3 0.8 reshape.201
  318.1 8.5 %all-to-all-done.1 = bf16[32,2,320]{2,1,0:T(2,128)(2,1)S(1)} async-done(((bf16[32,2,320]{2,1,0:T(2,128)(2,1)}), bf16[32,2,320]{2,1,0:T(2,128)(2,1)S(1)}, u32[]{:S(2)}, u32[]{:S(2)}) %all-to-all-start.1) | async-done | bytes 40992 | tf_op jit(solution)/shard_map/all_to_all | solution.py:86
  326.6 5.5 all-to-all-start
  332.8 1.3 dynamic-slice.1
  334.9 2.3 dynamic_update_slice.11
  337.3 2.3 dynamic_update_slice.10
  339.7 0.9 copy-done.8
  340.7 2.3 dynamic_update_slice.9
  344.6 104.8 %all-reduce.9.cloned.1.call-done = (f32[640,1,512]{2,1,0:T(1,128)}, f32[640,1,512]{2,1,0:T(1,128)}, f32[640,1,512]{2,1,0:T(1,128)}) async-done(((f32[640,1,512]{2,1,0:T(1,128)}, f32[640,1,512]{2,1,0:T(1,128)}, f32[640,1,512]{2,1,0:T(1,128)}), (f32[640,1,512]{2,1,0:T(1,128)}, f32[640,1,512]{2,1,0:T(1,128)}, f32[640,1,512]{2,1,0:T(1,128)})) %all-reduce.9.cloned.1.call-update) | async-done | bytes 3932176
  449.4 0.9 constant_dynamic-slice_fusion.10
  450.3 0.9 constant_dynamic-slice_fusion.9
  451.2 0.9 constant_dynamic-slice_fusion.8
  454.1 0.7 fusion.8
  455.3 0.7 fusion.5
  456.5 0.7 fusion.2
  457.2 2.0 pad_maximum_fusion
  459.2 0.7 pad_maximum_fusion.1
  459.9 285.6 %all-reduce.7.cloned.1.call-done = f32[3,512,512]{2,1,0:T(8,128)} async-done(((f32[3,512,512]{2,1,0:T(8,128)}), f32[3,512,512]{2,1,0:T(8,128)}) %all-reduce.7.cloned.1.call-update) | async-done | bytes 3145744 | tf_op jit(solution)/shard_map/psum | solution.py:109
  745.5 3.5 fusion.65
  749.1 1.3 copy.2028
  750.4 2.3 fusion.16
  752.7 1.0 fusion.9
  753.7 2.0 fusion.19
  755.8 1.1 constant_dynamic-slice_fusion
  757.0 3.3 convolution_bitcast_fusion.3
  760.3 1.1 constant_dynamic-slice_fusion.1
  761.5 0.9 fusion.54
  762.4 0.7 pad_maximum_fusion.2
  (174 shorter events, 10.4 us)
Async XLA Ops:
  7.2 191.9 %copy-start = (bf16[640,1280]{1,0:T(8,128)(2,1)S(1)}, bf16[640,1280]{1,0:T(8,128)(2,1)}, u32[]{:S(2)}) copy-start(bf16[640,1280]{1,0:T(8,128)(2,1)} %param.6) | copy-start | bytes 4915204
  7.2 191.9 %all-gather.4.cloned.1.call-start = ((), (), s32[]{:S(2)}) async-start(), calls=%async_computation.3 | async-start | bytes 1351680 | tf_op jit(solution)/shard_map/all_gather | solution.py:84
  53.5 4.0 copy-start.11
  53.5 4.0 copy-start.12
  58.9 162.8 %all-gather.6.cloned.1.call-start = ((), (), s32[]{:S(2)}) async-start(), calls=%async_computation.4 | async-start | bytes 1351680 | tf_op jit(solution)/shard_map/all_gather | solution.py:84
  174.8 135.6 %all-to-all-start.2 = ((bf16[32,2,320]{2,1,0:T(2,128)(2,1)}), bf16[32,2,320]{2,1,0:T(2,128)(2,1)S(1)}, u32[]{:S(2)}, u32[]{:S(2)}) async-start(bf16[32,2,320]{2,1,0:T(2,128)(2,1)} %reshape.197), calls=%async_computation.2 | async-start | bytes 98304 | tf_op jit(solution)/shard_map/all_to_all | solution.py:86
  189.5 115.2 %all-gather.8.cloned.1.call-start = ((), (), s32[]{:S(2)}) async-start(), calls=%async_computation.5 | async-start | bytes 1351680 | tf_op jit(solution)/shard_map/all_gather | solution.py:84
  192.1 257.3 %all-reduce.9.cloned.1.call-start = ((), (), s32[]{:S(2)}) async-start(), calls=%async_computation.7 | async-start | bytes 7864320
  309.4 23.0 %copy-start.10 = (f32[3,512,32]{1,2,0:T(8,128)S(1)}, f32[3,512,32]{1,2,0:T(8,128)}, u32[]{:S(2)}) copy-start(f32[3,512,32]{1,2,0:T(8,128)} %param.11) | copy-start | bytes 589828
  310.4 16.2 %all-to-all-start.1 = ((bf16[32,2,320]{2,1,0:T(2,128)(2,1)}), bf16[32,2,320]{2,1,0:T(2,128)(2,1)S(1)}, u32[]{:S(2)}, u32[]{:S(2)}) async-start(bf16[32,2,320]{2,1,0:T(2,128)(2,1)} %reshape.199), calls=%async_computation.1 | async-start | bytes 98304 | tf_op jit(solution)/shard_map/all_to_all | solution.py:86
  326.6 16.8 %all-to-all-start = ((bf16[32,2,320]{2,1,0:T(2,128)(2,1)}), bf16[32,2,320]{2,1,0:T(2,128)(2,1)S(1)}, u32[]{:S(2)}, u32[]{:S(2)}) async-start(bf16[32,2,320]{2,1,0:T(2,128)(2,1)} %reshape.201), calls=%async_computation | async-start | bytes 98304 | tf_op jit(solution)/shard_map/all_to_all | solution.py:86
  332.1 413.4 %all-reduce.7.cloned.1.call-start = ((), (), s32[]{:S(2)}) async-start(), calls=%async_computation.6 | async-start | bytes 6291456 | tf_op jit(solution)/shard_map/psum | solution.py:109
  337.2 2.4 copy-start.6
  339.6 1.0 copy-start.8
  340.7 111.4 %copy-start.2 = (bf16[2,512,512]{2,1,0:T(8,128)(2,1)S(1)}, bf16[2,512,512]{2,1,0:T(8,128)(2,1)}, u32[]{:S(2)}) copy-start(bf16[2,512,512]{2,1,0:T(8,128)(2,1)} %param.10) | copy-start | bytes 3145732
  343.1 1.0 copy-start.4
  452.8 1.2 copy-start.7
  454.1 1.2 copy-start.9
  455.3 1.2 copy-start.5
  750.4 2.3 copy-start.3
  757.0 6.1 copy-start.1
Sparse Core Ops, SparseCore 0:
  59.0 80.0 all-gather.3
  142.3 79.3 all-gather.5
  224.9 79.7 all-gather.7
  309.5 139.8 all-reduce.8
  459.3 286.1 all-reduce.6
